TPU v7x, 32 devices: a whole 2x2x4 slice. The times are simulated.
32 devices in a mesh: ctx: 8 (over z, y), head: 4 (over x, core).
Axes of the slice: x: 2, y: 2, z: 4, core: 2. Of those that a mesh axis runs over, the one named last changes fastest.
Arguments:
- queries: bfloat16 [16384, 3072], P('ctx', 'head'), may hold values from -11 to 11
- keys: bfloat16 [16384, 3072], P('ctx', 'head'), may hold values from -0.5 to 0.5
- values: bfloat16 [16384, 3072], P('ctx', 'head'), may hold values from -6 to 6
- documents: int32 [16384], P('ctx'), may hold values from 0 to 7, never falling along the last dimension, each value on 1 to 8192 neighbouring positions
- norm_gain: float32 [3072], P('head'), may hold values from 0.5 to 1.5
Outputs:
- normed: bfloat16 [16384, 3072], P('ctx', 'head')
Inputs may be any that keep to these rules, and one draw needn't show every extreme that they name: `documents`: document numbers never fall along the window; each document has 1 to 8192 tokens.
All inputs are finite; a program needn't handle non-finite values.
Results may differ from a plain program's by a relative error of at most 0.001.
Values sent between devices are 32-bit elements; how exact they have to be, the bound alone decides.
A program may use at most 128 MiB of HBM per device.

v0:
```python
import functools

import jax
import jax.numpy as jnp
from jax import lax
from jax.experimental import pallas as pl
from jax.experimental.pallas import tpu as pltpu
from jax.sharding import PartitionSpec as P

DH = 128
BLOCK = 256
EXTRA = 8
DOC_MOST = 8192
EPSILON = 1e-06
F32 = jnp.float32
BF16 = jnp.bfloat16


def split(x):
    high = x.astype(BF16)
    return high, (x - high.astype(F32)).astype(BF16)


def dot(a, b):
    return lax.dot_general(a, b, (((1,), (0,)), ((), ())), preferred_element_type=F32)


def dot_nt(a, b):
    return lax.dot_general(a, b, (((1,), (1,)), ((), ())), preferred_element_type=F32)


def dot_tn(a, b):
    return lax.dot_general(a, b, (((0,), (0,)), ((), ())), preferred_element_type=F32)


def eye_mask():
    return lax.broadcasted_iota(jnp.int32, (BLOCK, BLOCK), 0) == lax.broadcasted_iota(
        jnp.int32, (BLOCK, BLOCK), 1
    )


def to_column(row):
    return jnp.sum(jnp.where(eye_mask(), row, 0.0), axis=1, keepdims=True)


def to_row(column):
    return jnp.sum(jnp.where(eye_mask(), column, 0.0), axis=0, keepdims=True)


def state_kernel(heads, blocks, k_ref, v_ref, d_ref, msg_ref):
    last = d_ref[blocks - 1 : blocks, BLOCK - 1 : BLOCK]
    totals = [None] * heads
    for b in range(blocks):
        tail = to_column(d_ref[b : b + 1, :]) == last
        rows = slice(b * BLOCK, (b + 1) * BLOCK)
        for h in range(heads):
            cols = slice(h * DH, (h + 1) * DH)
            key = jnp.where(tail, k_ref[rows, cols], jnp.zeros((), BF16))
            part = dot_tn(key, v_ref[rows, cols])
            totals[h] = part if totals[h] is None else totals[h] + part
    for h in range(heads):
        msg_ref[h, :DH, :] = totals[h]
        msg_ref[h, DH:, :] = jnp.broadcast_to(last, (EXTRA, DH))


def main_kernel(heads, q_ref, k_ref, v_ref, d_ref, o_ref, state, mark):
    b = pl.program_id(0)

    @pl.when(b == 0)
    def _():
        state[...] = jnp.zeros_like(state)
        mark[...] = jnp.zeros_like(mark)

    row = d_ref[0]
    column = to_column(row)
    causal = lax.broadcasted_iota(jnp.int32, (BLOCK, BLOCK), 0) >= lax.broadcasted_iota(
        jnp.int32, (BLOCK, BLOCK), 1
    )
    keep = causal & (column == row)
    before = mark[0:1, 0:1]
    live = column == before
    last = row[:, BLOCK - 1 : BLOCK]
    tail = column == last
    same = before == last
    for h in range(heads):
        cols = slice(h * DH, (h + 1) * DH)
        query, key, value = q_ref[:, cols], k_ref[:, cols], v_ref[:, cols]
        high, low = split(jnp.where(keep, dot_nt(query, key), 0.0))
        old = state[h]
        old_high, old_low = split(old)
        carried = dot(query, old_high) + dot(query, old_low)
        o_ref[:, cols] = dot(high, value) + dot(low, value) + jnp.where(live, carried, 0.0)
        fresh = dot_tn(jnp.where(tail, key, jnp.zeros((), BF16)), value)
        state[h] = fresh + jnp.where(same, old, 0.0)
    mark[...] = jnp.broadcast_to(last, mark.shape)


def correct_kernel(heads, a_ref, q_ref, d_ref, m_ref, o_ref, s_ref):
    column = to_column(d_ref[0])
    total = jnp.zeros((BLOCK, DH), F32)
    for h in range(heads):
        cols = slice(h * DH, (h + 1) * DH)
        high, low = split(m_ref[h, :DH, :])
        live = column == m_ref[h, DH : DH + 1, 0:1]
        query = q_ref[:, cols]
        whole = a_ref[:, cols] + jnp.where(live, dot(query, high) + dot(query, low), 0.0)
        o_ref[:, cols] = whole
        total = total + whole * whole
    s_ref[0] = to_row(jnp.sum(total, axis=1, keepdims=True))


def final_kernel(scale, a_ref, s_ref, g_ref, o_ref):
    factor = to_column(lax.rsqrt(s_ref[0] * scale + EPSILON))
    o_ref[...] = (a_ref[...] * factor * g_ref[...]).astype(BF16)


def join(newer, older):
    same = newer[:, DH : DH + 1, 0:1] == older[:, DH : DH + 1, 0:1]
    held = newer[:, :DH] + jnp.where(same, older[:, :DH], 0.0)
    return jnp.concatenate([held, newer[:, DH:]], axis=1)


def shards(queries, keys, values, documents, norm_gain):
    row_count, width = queries.shape
    heads = width // DH
    half = heads // 2
    blocks = row_count // BLOCK
    n = lax.axis_size("ctx")
    odd = lax.axis_index("ctx") % 2 == 1
    docs = (documents + 1).astype(F32).reshape(blocks, BLOCK)
    docs3 = docs.reshape(blocks, 1, BLOCK)
    params = pltpu.CompilerParams(vmem_limit_bytes=48 * 1024 * 1024)
    msg = pl.pallas_call(
        functools.partial(state_kernel, heads, blocks),
        out_shape=jax.ShapeDtypeStruct((heads, DH + EXTRA, DH), F32),
        compiler_params=params,
    )(keys, values, docs)
    swap = [(i, i ^ 1) for i in range(n)]
    ahead = [(i, i + 2) for i in range(n - 2)]
    own = jnp.where(odd, msg[half:], msg[:half])
    other = jnp.where(odd, msg[:half], msg[half:])
    got = lax.ppermute(other, "ctx", swap)
    first, second = jnp.where(odd, got, own), jnp.where(odd, own, got)
    steps = -(-(DOC_MOST - 1) // (2 * row_count))
    travel = join(second, first)
    reach = None
    for _ in range(steps):
        travel = lax.ppermute(travel, "ctx", ahead)
        reach = travel if reach is None else join(reach, travel)
    for_odd = join(first, reach)
    keep, give = jnp.where(odd, for_odd, reach), jnp.where(odd, reach, for_odd)
    got = lax.ppermute(give, "ctx", swap)
    incoming = jnp.concatenate([jnp.where(odd, got, keep), jnp.where(odd, keep, got)], axis=0)

    wide = pl.BlockSpec((BLOCK, width), lambda b: (b, 0))
    line = pl.BlockSpec((1, 1, BLOCK), lambda b: (b, 0, 0))
    local = pl.pallas_call(
        functools.partial(main_kernel, heads),
        grid=(blocks,),
        in_specs=[wide, wide, wide, line],
        out_specs=wide,
        out_shape=jax.ShapeDtypeStruct((row_count, width), F32),
        scratch_shapes=[pltpu.VMEM((heads, DH, DH), F32), pltpu.VMEM((8, DH), F32)],
        compiler_params=params,
        cost_estimate=pl.CostEstimate(
            flops=row_count * width * 2000, bytes_accessed=row_count * width * 10, transcendentals=0
        ),
    )(queries, keys, values, docs3)
    whole, squares = pl.pallas_call(
        functools.partial(correct_kernel, heads),
        grid=(blocks,),
        in_specs=[wide, wide, line, pl.BlockSpec((heads, DH + EXTRA, DH), lambda b: (0, 0, 0))],
        out_specs=[wide, line],
        out_shape=[
            jax.ShapeDtypeStruct((row_count, width), F32),
            jax.ShapeDtypeStruct((blocks, 1, BLOCK), F32),
        ],
        compiler_params=params,
    )(local, queries, docs3, incoming)
    total = lax.psum(squares, "head")
    scale = 1.0 / (width * lax.axis_size("head"))
    return pl.pallas_call(
        functools.partial(final_kernel, scale),
        grid=(blocks,),
        in_specs=[wide, line, pl.BlockSpec((1, width), lambda b: (0, 0))],
        out_specs=wide,
        out_shape=jax.ShapeDtypeStruct((row_count, width), BF16),
        compiler_params=params,
    )(whole, total, norm_gain[None, :])


def solution(mesh):
    return jax.shard_map(
        shards,
        mesh=mesh,
        in_specs=(P("ctx", "head"), P("ctx", "head"), P("ctx", "head"), P("ctx"), P("head")),
        out_specs=P("ctx", "head"),
        check_vma=False,
    )
```

profile of v0, /device:TPU:9, one launch (start us, length us, event | category | flops | bytes accessed | tf_op | source)
XLA Modules:
  0.0 66.8 jit_solution(3548351417733325286)
XLA Ops:
  0.0 0.7 %add_convert_fusion = f32[2048]{0:T(1024)S(1)} fusion(s32[2048]{0:T(1024)} %param.8), kind=kLoop, calls=%fused_computation.16 | loop fusion | flops 4096 | bytes 16384 | tf_op jit(solution)/shard_map/convert_element_type | solution.py:130
  0.7 0.0 copy-start
  0.7 1.9 %copy-done = bf16[2048,768]{1,0:T(8,128)(2,1)S(1)} copy-done((bf16[2048,768]{1,0:T(8,128)(2,1)S(1)}, bf16[2048,768]{1,0:T(8,128)(2,1)}, u32[]{:S(2)}) %copy-start) | copy-done | bytes 3145752
  2.6 0.0 copy-start.2
  2.6 3.7 %shard_map.56 = f32[6,136,128]{2,1,0:T(8,128)S(1)} custom-call(bf16[2048,768]{1,0:T(8,128)(2,1)S(1)} %copy-done, bf16[2048,768]{1,0:T(8,128)(2,1)} %v_ref.3, f32[8,256]{1,0:T(8,128)S(1)} %reshape.3.d_ref), custom_call_target="tpu_custom_call" | custom-call | tf_op jit(solution)/shard_map/pallas_call | solution.py:133
  6.3 0.0 copy-start.1
  6.3 1.3 %collective-permute-start = (f32[3,136,128]{2,1,0:T(8,128)S(1)}, f32[3,136,128]{2,1,0:T(8,128)S(1)}, u32[]{:S(2)}, u32[]{:S(2)}) collective-permute-start(f32[3,136,128]{2,1,0:T(8,128)S(1)} %slice_select_fusion.1), channel_id=1, source_target_pairs={{0,4},{4,0},{8,12},{12,8},{16,20},{20,16},{24,28},{28,24},{1,5},{5... | collective-permute-start | bytes 626696 | tf_op jit(solution)/shard_map/ppermute | solution.py:142
  7.6 4.8 %collective-permute-done = f32[3,136,128]{2,1,0:T(8,128)S(1)} collective-permute-done((f32[3,136,128]{2,1,0:T(8,128)S(1)}, f32[3,136,128]{2,1,0:T(8,128)S(1)}, u32[]{:S(2)}, u32[]{:S(2)}) %collective-permute-start) | collective-permute-done | bytes 208928 | tf_op jit(solution)/shard_map/ppermute | solution.py:142
  12.5 0.2 compare_reduce_fusion.2
  12.6 0.1 slice_add_fusion
  12.8 3.2 %collective-permute-start.1 = (f32[3,136,128]{2,1,0:T(8,128)S(1)}, f32[3,136,128]{2,1,0:T(8,128)S(1)}, u32[]{:S(2)}, u32[]{:S(2)}) collective-permute-start(f32[3,136,128]{2,1,0:T(8,128)S(1)} %pad_maximum_fusion.1), channel_id=1, source_target_pairs={{0,8},{4,12},{8,16},{12,20},{16,24},{20,28},{1,9},{5,13},{9,17},{1... | collective-permute-start | bytes 626696 | tf_op jit(solution)/shard_map/ppermute | solution.py:148
  16.0 3.8 %collective-permute-done.1 = f32[3,136,128]{2,1,0:T(8,128)S(1)} collective-permute-done((f32[3,136,128]{2,1,0:T(8,128)S(1)}, f32[3,136,128]{2,1,0:T(8,128)S(1)}, u32[]{:S(2)}, u32[]{:S(2)}) %collective-permute-start.1) | collective-permute-done | bytes 208928 | tf_op jit(solution)/shard_map/ppermute | solution.py:148
  19.8 3.2 %collective-permute-start.2 = (f32[3,136,128]{2,1,0:T(8,128)S(1)}, f32[3,136,128]{2,1,0:T(8,128)S(1)}, u32[]{:S(2)}, u32[]{:S(2)}) collective-permute-start(f32[3,136,128]{2,1,0:T(8,128)S(1)} %collective-permute-done.1), channel_id=1, source_target_pairs={{0,8},{4,12},{8,16},{12,20},{16,24},{20,28},{1,9},{5,13},{9,17},{1... | collective-permute-start | bytes 626696 | tf_op jit(solution)/shard_map/ppermute | solution.py:148
  23.0 0.0 copy-done.2
  23.0 3.3 %collective-permute-done.2 = f32[3,136,128]{2,1,0:T(8,128)S(1)} collective-permute-done((f32[3,136,128]{2,1,0:T(8,128)S(1)}, f32[3,136,128]{2,1,0:T(8,128)S(1)}, u32[]{:S(2)}, u32[]{:S(2)}) %collective-permute-start.2) | collective-permute-done | bytes 208928 | tf_op jit(solution)/shard_map/ppermute | solution.py:148
  26.3 0.2 compare_reduce_fusion
  26.5 0.1 select_add_fusion
  26.7 1.3 %collective-permute-start.3 = (f32[3,136,128]{2,1,0:T(8,128)S(1)}, f32[3,136,128]{2,1,0:T(8,128)S(1)}, u32[]{:S(2)}, u32[]{:S(2)}) collective-permute-start(f32[3,136,128]{2,1,0:T(8,128)S(1)} %fusion.2), channel_id=1, source_target_pairs={{0,4},{4,0},{8,12},{12,8},{16,20},{20,16},{24,28},{28,24},{1,5},{5... | collective-permute-start | bytes 626696 | tf_op jit(solution)/shard_map/ppermute | solution.py:152
  28.0 0.0 copy-done.1
  28.0 13.8 %shard_map.55.a_ref = f32[2048,768]{1,0:T(8,128)} custom-call(bf16[2048,768]{1,0:T(8,128)(2,1)S(1)} %copy-done.1, bf16[2048,768]{1,0:T(8,128)(2,1)} %k_ref.3, bf16[2048,768]{1,0:T(8,128)(2,1)} %v_ref.3, f32[8,1,256]{2,1,0:T(1,128)S(1)} %bitcast.1), custom_call_target="tpu_custom_call" | custom-call | flops 3145728000 | bytes 15728640 | tf_op jit(solution)/shard_map/pallas_call | solution.py:157
  41.8 0.0 collective-permute-done.3
  41.8 0.1 broadcast_select_fusion.1
  41.9 8.8 %shard_map.57 = (f32[2048,768]{1,0:T(8,128)}, f32[8,1,256]{2,1,0:T(1,128)S(1)}) custom-call(f32[2048,768]{1,0:T(8,128)} %shard_map.55.a_ref, bf16[2048,768]{1,0:T(8,128)(2,1)S(1)} %copy-done.1, f32[8,1,256]{2,1,0:T(1,128)S(1)} %bitcast.2, f32[6,136,128]{2,1,0:T(8,128)S(1)} %pad_maximum_fusion.m_ref), custom_call_target="tpu_custom_call" | custom-call | tf_op jit(solution)/shard_map/pallas_call | solution.py:169
  50.7 8.9 %psum.7.s_ref = f32[8,1,256]{2,1,0:T(1,128)S(1)} all-reduce(f32[8,1,256]{2,1,0:T(1,128)S(1)} %get-tuple-element.8), channel_id=1, replica_groups=mesh['ctx'=8,'head'=4] {'head'}, use_global_device_ids=true, to_apply=%region_0.1 | all-reduce | flops 2048 | bytes 16384 | tf_op jit(solution)/shard_map/psum | solution.py:180
  59.6 7.2 %shard_map.58 = bf16[2048,768]{1,0:T(8,128)(2,1)} custom-call(f32[2048,768]{1,0:T(8,128)} %get-tuple-element.7.a_ref, f32[8,1,256]{2,1,0:T(1,128)S(1)} %psum.7.s_ref, f32[1,768]{1,0:T(1,128)S(1)} %broadcast_in_dim.40.g_ref), custom_call_target="tpu_custom_call" | custom-call | tf_op jit(solution)/shard_map/pallas_call | solution.py:182
  (10 shorter events, 0.2 us)
Async XLA Ops:
  0.7 1.9 %copy-start = (bf16[2048,768]{1,0:T(8,128)(2,1)S(1)}, bf16[2048,768]{1,0:T(8,128)(2,1)}, u32[]{:S(2)}) copy-start(bf16[2048,768]{1,0:T(8,128)(2,1)} %k_ref.3) | copy-start | bytes 9437188
  2.6 20.4 %copy-start.2 = (f32[768]{0:T(1024)S(1)}, f32[768]{0:T(1024)}, u32[]{:S(2)}) copy-start(f32[768]{0:T(1024)} %param.9) | copy-start | bytes 9220
  6.3 21.7 %copy-start.1 = (bf16[2048,768]{1,0:T(8,128)(2,1)S(1)}, bf16[2048,768]{1,0:T(8,128)(2,1)}, u32[]{:S(2)}) copy-start(bf16[2048,768]{1,0:T(8,128)(2,1)} %q_ref.3) | copy-start | bytes 9437188
  6.3 6.1 %collective-permute-start = (f32[3,136,128]{2,1,0:T(8,128)S(1)}, f32[3,136,128]{2,1,0:T(8,128)S(1)}, u32[]{:S(2)}, u32[]{:S(2)}) collective-permute-start(f32[3,136,128]{2,1,0:T(8,128)S(1)} %slice_select_fusion.1), channel_id=1, source_target_pairs={{0,4},{4,0},{8,12},{12,8},{16,20},{20,16},{24,28},{28,24},{1,5},{5... | collective-permute-start | bytes 626696 | tf_op jit(solution)/shard_map/ppermute | solution.py:142
  12.8 7.0 %collective-permute-start.1 = (f32[3,136,128]{2,1,0:T(8,128)S(1)}, f32[3,136,128]{2,1,0:T(8,128)S(1)}, u32[]{:S(2)}, u32[]{:S(2)}) collective-permute-start(f32[3,136,128]{2,1,0:T(8,128)S(1)} %pad_maximum_fusion.1), channel_id=1, source_target_pairs={{0,8},{4,12},{8,16},{12,20},{16,24},{20,28},{1,9},{5,13},{9,17},{1... | collective-permute-start | bytes 626696 | tf_op jit(solution)/shard_map/ppermute | solution.py:148
  19.8 6.5 %collective-permute-start.2 = (f32[3,136,128]{2,1,0:T(8,128)S(1)}, f32[3,136,128]{2,1,0:T(8,128)S(1)}, u32[]{:S(2)}, u32[]{:S(2)}) collective-permute-start(f32[3,136,128]{2,1,0:T(8,128)S(1)} %collective-permute-done.1), channel_id=1, source_target_pairs={{0,8},{4,12},{8,16},{12,20},{16,24},{20,28},{1,9},{5,13},{9,17},{1... | collective-permute-start | bytes 626696 | tf_op jit(solution)/shard_map/ppermute | solution.py:148
  26.7 15.1 %collective-permute-start.3 = (f32[3,136,128]{2,1,0:T(8,128)S(1)}, f32[3,136,128]{2,1,0:T(8,128)S(1)}, u32[]{:S(2)}, u32[]{:S(2)}) collective-permute-start(f32[3,136,128]{2,1,0:T(8,128)S(1)} %fusion.2), channel_id=1, source_target_pairs={{0,4},{4,0},{8,12},{12,8},{16,20},{20,16},{24,28},{28,24},{1,5},{5... | collective-permute-start | bytes 626696 | tf_op jit(solution)/shard_map/ppermute | solution.py:152
where the time goes:
time: 68 us; the launch traced here: 66.8 us
  Pallas kernels  33.5 us (49%)
  waiting for transfers between devices  11.8 us (17%)
  starting transfers between devices  9.03 us (13%)
  blocking collectives  8.92 us (13%)
  local copies, waits for them, and re-layouts  1.92 us (3%)
  other arithmetic  1.46 us (2%)
    pallas_call x1, Pallas kernels, shards(): pl.pallas_call(functools.partial(main_kernel, heads), grid=(blocks,), in_...  13.8 us
    psum x1, blocking collectives, shards(): total = lax.psum(squares, 'head')  8.92 us
    pallas_call x1, Pallas kernels, shards(): pl.pallas_call(functools.partial(correct_kernel, heads), grid=(blocks,),...  8.79 us
    pallas_call x1, Pallas kernels, shards(): pl.pallas_call(functools.partial(final_kernel, scale), grid=(blocks,), in...  7.24 us
    ppermute x2, waiting for transfers between devices, shards(): travel = lax.ppermute(travel, 'ctx', ahead)  7.06 us
    ppermute x2, starting transfers between devices, shards(): travel = lax.ppermute(travel, 'ctx', ahead)  6.42 us
    ppermute x1, waiting for transfers between devices, shards(): got = lax.ppermute(other, 'ctx', swap)  4.79 us
    pallas_call x1, Pallas kernels, shards(): pl.pallas_call(functools.partial(state_kernel, heads, blocks), out_shape=...  3.68 us
  transfers between devices with their start and end apart: 4, of which 3 were waited for; matrix products, arithmetic and copies ran while one was open for 0% of the time, Pallas kernels for 21%

commit v1 on v0

v1 whole, which is shorter than its diff:
```python
import functools

import jax
import jax.numpy as jnp
from jax import lax
from jax.experimental import pallas as pl
from jax.experimental.pallas import tpu as pltpu
from jax.sharding import PartitionSpec as P

DH = 128
BLOCK = 256
EXTRA = 8
DOC_MOST = 8192
EPSILON = 1e-06
F32 = jnp.float32
BF16 = jnp.bfloat16


def split(x):
    high = x.astype(BF16)
    return high, (x - high.astype(F32)).astype(BF16)


def dot(a, b):
    return lax.dot_general(a, b, (((1,), (0,)), ((), ())), preferred_element_type=F32)


def dot_nt(a, b):
    return lax.dot_general(a, b, (((1,), (1,)), ((), ())), preferred_element_type=F32)


def dot_tn(a, b):
    return lax.dot_general(a, b, (((0,), (0,)), ((), ())), preferred_element_type=F32)


def eye_mask():
    return lax.broadcasted_iota(jnp.int32, (BLOCK, BLOCK), 0) == lax.broadcasted_iota(
        jnp.int32, (BLOCK, BLOCK), 1
    )


def to_column(row):
    return jnp.sum(jnp.where(eye_mask(), row, 0.0), axis=1, keepdims=True)


def to_row(column):
    return jnp.sum(jnp.where(eye_mask(), column, 0.0), axis=0, keepdims=True)


def join(newer, older):
    same = newer[DH : DH + 1, 0:1] == older[DH : DH + 1, 0:1]
    return newer[:DH] + jnp.where(same, older[:DH], 0.0), newer[DH:]


def carry_in(query, pair):
    both = dot(query, pair)
    return both[:, :DH] + both[:, DH:]


def fused_kernel(heads, blocks, steps, n, nh, scale, *refs):
    (q_ref, k_ref, v_ref, d_ref, g_ref, o_ref, whole, state, mark, sent, got, travel, give, back,
     incoming, pairs, squares, others, send_a, recv_a, send_t, recv_t, send_b, recv_b, send_s,
     recv_s) = refs
    half = heads // 2
    me, place = lax.axis_index("ctx"), lax.axis_index("head")
    odd = lax.rem(me, 2)
    is_odd = odd == 1
    partner = me + 1 - 2 * odd
    ahead = lax.rem(me + 2, n)
    behind = lax.rem(me + n - 2, n)
    has_next, has_prev = me < n - 2, me >= 2
    own, other = odd * half, (1 - odd) * half

    def copy(source, target, send, recv, ctx, head):
        return pltpu.make_async_remote_copy(
            src_ref=source,
            dst_ref=target,
            send_sem=send,
            recv_sem=recv,
            device_id=(ctx, head),
            device_id_type=pl.DeviceIdType.MESH,
        )

    barrier = pltpu.get_barrier_semaphore()

    def greet(ctx, head):
        pl.semaphore_signal(
            barrier, inc=1, device_id=(ctx, head), device_id_type=pl.DeviceIdType.MESH
        )

    greet(partner, place)
    for j in range(1, nh):
        greet(me, lax.rem(place + j, nh))

    greet(ahead, place)
    greet(behind, place)

    last = d_ref[blocks - 1][:, BLOCK - 1 : BLOCK]
    tails = [to_column(d_ref[b]) == last for b in range(blocks)]

    def local_state(h):
        cols = pl.ds(pl.multiple_of(h * DH, DH), DH)
        total = None
        for b in range(blocks):
            rows = slice(b * BLOCK, (b + 1) * BLOCK)
            key = jnp.where(tails[b], k_ref[rows, cols], jnp.zeros((), BF16))
            part = dot_tn(key, v_ref[rows, cols])
            total = part if total is None else total + part
        sent[h, :DH, :] = total
        sent[h, DH:, :] = jnp.broadcast_to(last, (EXTRA, DH))

    swap_a = [
        copy(sent.at[other + i], got.at[i], send_a.at[i], recv_a.at[i], partner, place)
        for i in range(half)
    ]
    hops = [
        [
            copy(
                travel.at[t, i], travel.at[t + 1, i], send_t.at[t, i], recv_t.at[t, i], ahead, place
            )
            for i in range(half)
        ]
        for t in range(steps)
    ]
    swap_b = [
        copy(give.at[i], back.at[i], send_b.at[i], recv_b.at[i], partner, place)
        for i in range(half)
    ]
    for i in range(half):
        local_state(other + i)
        if i == 0:
            pl.semaphore_wait(barrier, nh + 2)
        swap_a[i].start()
    for i in range(half):
        local_state(own + i)

    @pl.when(me < 2)
    def _():
        for t in range(steps):
            travel[t + 1] = jnp.zeros((half, DH + EXTRA, DH), F32)

    state[...] = jnp.zeros_like(state)
    mark[...] = jnp.zeros_like(mark)
    causal = lax.broadcasted_iota(jnp.int32, (BLOCK, BLOCK), 0) >= lax.broadcasted_iota(
        jnp.int32, (BLOCK, BLOCK), 1
    )

    def block_step(b, carry):
        rows = pl.ds(pl.multiple_of(b * BLOCK, BLOCK), BLOCK)
        row = d_ref[b]
        column = to_column(row)
        keep = causal & (column == row)
        before = mark[0:1, 0:1]
        live = column == before
        final = row[:, BLOCK - 1 : BLOCK]
        tail = column == final
        same = before == final
        for h in range(heads):
            cols = slice(h * DH, (h + 1) * DH)
            query, key, value = q_ref[rows, cols], k_ref[rows, cols], v_ref[rows, cols]
            high, low = split(jnp.where(keep, dot_nt(query, key), 0.0))
            old = state[h]
            carried = carry_in(query, jnp.concatenate(split(old), axis=1))
            whole[rows, cols] = dot(high, value) + dot(low, value) + jnp.where(live, carried, 0.0)
            fresh = dot_tn(jnp.where(tail, key, jnp.zeros((), BF16)), value)
            state[h] = fresh + jnp.where(same, old, 0.0)
        mark[...] = jnp.broadcast_to(final, mark.shape)
        return carry

    def first_of(i):
        return jnp.where(is_odd, got[i], sent[own + i])

    cuts = [(blocks * j) // (steps + 2) for j in range(steps + 3)]
    lax.fori_loop(cuts[0], cuts[1], block_step, 0)
    for i in range(half):
        swap_a[i].wait_recv()
        held, tag = join(jnp.where(is_odd, sent[own + i], got[i]), first_of(i))
        travel[0, i, :DH, :] = held
        travel[0, i, DH:, :] = tag

        @pl.when(has_next)
        def _():
            hops[0][i].start()

    for t in range(1, steps):
        lax.fori_loop(cuts[t], cuts[t + 1], block_step, 0)
        for i in range(half):

            @pl.when(has_prev)
            def _():
                hops[t - 1][i].wait_recv()

            @pl.when(has_next)
            def _():
                hops[t][i].start()

    lax.fori_loop(cuts[steps], cuts[steps + 1], block_step, 0)
    for i in range(half):

        @pl.when(has_prev)
        def _():
            hops[steps - 1][i].wait_recv()

        reach = travel[1, i]
        for t in range(1, steps):
            reach = jnp.concatenate(join(reach, travel[t + 1, i]), axis=0)
        for_odd = jnp.concatenate(join(first_of(i), reach), axis=0)
        give[i] = jnp.where(is_odd, reach, for_odd)
        swap_b[i].start()
        incoming[own + i] = jnp.where(is_odd, for_odd, reach)
    lax.fori_loop(cuts[steps + 1], cuts[steps + 2], block_step, 0)
    for i in range(half):
        swap_b[i].wait_recv()
        incoming[other + i] = back[i]
    for h in range(heads):
        pairs[h] = jnp.concatenate(split(incoming[h, :DH, :]), axis=1)
    target = incoming[0, DH : DH + 1, 0:1]

    def correct_step(b, carry):
        rows = pl.ds(pl.multiple_of(b * BLOCK, BLOCK), BLOCK)
        live = to_column(d_ref[b]) == target
        total = jnp.zeros((BLOCK, DH), F32)
        for h in range(heads):
            cols = slice(h * DH, (h + 1) * DH)
            fixed = whole[rows, cols] + jnp.where(live, carry_in(q_ref[rows, cols], pairs[h]), 0.0)
            whole[rows, cols] = fixed
            total = total + fixed * fixed
        squares[b] = to_row(jnp.sum(total, axis=1, keepdims=True))
        return carry

    lax.fori_loop(0, blocks, correct_step, 0)
    sums = [
        copy(
            squares,
            others.at[j - 1],
            send_s.at[j - 1],
            recv_s.at[j - 1],
            me,
            lax.rem(place + j, nh),
        )
        for j in range(1, nh)
    ]
    for item in sums:
        item.start()
    for item in sums:
        item.wait_recv()

    def final_step(b, carry):
        rows = pl.ds(pl.multiple_of(b * BLOCK, BLOCK), BLOCK)
        total = squares[b]
        for j in range(nh - 1):
            total = total + others[j, b]
        factor = to_column(lax.rsqrt(total * scale + EPSILON))
        for h in range(heads):
            cols = slice(h * DH, (h + 1) * DH)
            o_ref[rows, cols] = (whole[rows, cols] * factor * g_ref[:, cols]).astype(BF16)
        return carry

    lax.fori_loop(0, blocks, final_step, 0)
    for item in swap_a + swap_b + sums:
        item.wait_send()

    @pl.when(has_next)
    def _():
        for hop in hops:
            for item in hop:
                item.wait_send()


def shards(queries, keys, values, documents, norm_gain):
    row_count, width = queries.shape
    heads = width // DH
    half = heads // 2
    blocks = row_count // BLOCK
    n, nh = lax.axis_size("ctx"), lax.axis_size("head")
    steps = -(-(DOC_MOST - 1) // (2 * row_count))
    docs = (documents + 1).astype(F32).reshape(blocks, 1, BLOCK)
    message = (DH + EXTRA, DH)
    dma = pltpu.SemaphoreType.DMA
    vmem = pl.BlockSpec(memory_space=pltpu.VMEM)
    return pl.pallas_call(
        functools.partial(fused_kernel, heads, blocks, steps, n, nh, 1.0 / (width * nh)),
        in_specs=[vmem] * 5,
        out_specs=vmem,
        out_shape=jax.ShapeDtypeStruct((row_count, width), BF16),
        scratch_shapes=[
            pltpu.VMEM((row_count, width), F32),
            pltpu.VMEM((heads, DH, DH), F32),
            pltpu.VMEM((8, DH), F32),
            pltpu.VMEM((heads, *message), F32),
            pltpu.VMEM((half, *message), F32),
            pltpu.VMEM((steps + 1, half, *message), F32),
            pltpu.VMEM((half, *message), F32),
            pltpu.VMEM((half, *message), F32),
            pltpu.VMEM((heads, *message), F32),
            pltpu.VMEM((heads, DH, 2 * DH), BF16),
            pltpu.VMEM((blocks, 1, BLOCK), F32),
            pltpu.VMEM((nh - 1, blocks, 1, BLOCK), F32),
            dma((half,)),
            dma((half,)),
            dma((steps, half)),
            dma((steps, half)),
            dma((half,)),
            dma((half,)),
            dma((nh - 1,)),
            dma((nh - 1,)),
        ],
        compiler_params=pltpu.CompilerParams(
            vmem_limit_bytes=56 * 1024 * 1024, collective_id=0, has_side_effects=True
        ),
    )(queries, keys, values, docs, norm_gain[None, :])


def solution(mesh):
    return jax.shard_map(
        shards,
        mesh=mesh,
        in_specs=(P("ctx", "head"), P("ctx", "head"), P("ctx", "head"), P("ctx"), P("head")),
        out_specs=P("ctx", "head"),
        check_vma=False,
    )
```

time: 68 us -> 43.8 us (0.64); the launches traced: 66.8 us -> 43.6 us
  waiting for transfers between devices: 11.8 us -> 0 us
  starting transfers between devices: 9.03 us -> 0 us
  blocking collectives: 8.92 us -> 0 us
  Pallas kernels: 33.5 us -> 37.3 us
  local copies, waits for them, and re-layouts: 1.92 us -> 5.02 us
    ppermute x4 -> x0, waiting for transfers between devices: 11.8 us -> none  [the longest x2 7.06 us: shards(): travel = lax.ppermute(travel, 'ctx', ahead)]
    ppermute x4 -> x0, starting transfers between devices: 9.03 us -> none  [the longest x2 6.42 us: shards(): travel = lax.ppermute(travel, 'ctx', ahead)]
    psum x1 -> x0, blocking collectives: 8.92 us -> none  [shards(): total = lax.psum(squares, 'head')]
    pallas_call x4 -> x1, Pallas kernels: 33.5 us -> 37.3 us  [shards(): pl.pallas_call(functools.partial(fused_kernel, heads, blocks, steps, n, n...]
    unnamed x6 -> x1, local copies, waits for them, and re-layouts: 1.9 us -> 3.76 us
    broadcast_in_dim x1, local copies, waits for them, and re-layouts: 0.01 us -> 1.27 us  [shards(): norm_gain[None, :]]
  transfers between devices with their start and end apart: 4 -> 0, of which waited for: 3 -> 0; matrix products, arithmetic and copies ran while one was open for 0% -> 0% of each run, Pallas kernels for 21% -> 0%
where the time goes in v1:
time: 43.8 us; the launch traced here: 43.6 us
  Pallas kernels  37.3 us (85%)
  local copies, waits for them, and re-layouts  5.02 us (11%)
  other arithmetic  1.3 us (3%)
    pallas_call x1, Pallas kernels, shards(): pl.pallas_call(functools.partial(fused_kernel, heads, blocks, steps, n, n...  37.3 us
    unnamed x1, local copies, waits for them, and re-layouts  3.76 us
    convert_element_type x1, other arithmetic, shards(): docs = (documents + 1).astype(F32).reshape(blocks, 1, BLOCK)  1.3 us
    broadcast_in_dim x1, local copies, waits for them, and re-layouts, shards(): norm_gain[None, :]  1.27 us

profile of v1, /device:TPU:9, one launch (start us, length us, event | category | flops | bytes accessed | tf_op | source)
XLA Modules:
  0.0 43.6 jit_solution(365799761541411830)
XLA Ops:
  0.0 1.3 %broadcast_in_dim.3.refs_4_ = f32[1,768]{1,0:T(1,128)} reshape(f32[768]{0:T(1024)} %param.9) | data formatting | bytes 6144 | tf_op jit(solution)/shard_map/broadcast_in_dim | solution.py:311
  1.3 1.3 %add_convert_fusion = f32[2048]{0:T(1024)} fusion(s32[2048]{0:T(1024)} %param.8), kind=kLoop, calls=%fused_computation | loop fusion | flops 4096 | bytes 16384 | tf_op jit(solution)/shard_map/convert_element_type | solution.py:277
  2.6 37.3 %shard_map.55 = bf16[2048,768]{1,0:T(8,128)(2,1)} custom-call(bf16[2048,768]{1,0:T(8,128)(2,1)} %refs_0_.1, bf16[2048,768]{1,0:T(8,128)(2,1)} %refs_1_.1, bf16[2048,768]{1,0:T(8,128)(2,1)} %refs_2_.1, f32[8,1,256]{2,1,0:T(1,128)} %bitcast.1, f32[1,768]{1,0:T(1,128)} %broadcast_in_dim.3.refs_4_), custom_call_target="tpu_custom_call" | custom-call | tf_op jit(solution)/shard_map/pallas_call | solution.py:281
  39.8 3.8 %copy.7 = bf16[2048,768]{1,0:T(8,128)(2,1)} copy(bf16[2048,768]{1,0:T(8,128)(2,1)} %shard_map.55) | data formatting | bytes 6291456
